TPU v7x, 32 devices: a whole 2x2x4 slice. The times are simulated.
32 devices in a mesh: bl: 4 (over y, x), freq: 8 (over z, core).
Axes of the slice: x: 2, y: 2, z: 4, core: 2. Of those that a mesh axis runs over, the one named last changes fastest.
Arguments:
- visibilities: float32 [2, 2, 128, 8192], P(None, None, 'freq', 'bl'), may hold values from -8 to 8
- sample_flag_weight: int32 [2, 128, 8192], P(None, 'freq', 'bl'), may hold values from 0 to 4
- baseline_station_pair: int32 [2, 8192], P(None, 'bl'), may hold values from 0 to 511, as said below
- baseline_spatial_coords: float32 [2, 2, 8192], P(None, None, 'bl'), may hold values from -6 to 6
- directions: float32 [2, 8], replicated, may hold values from -0.5 to 0.5
- source_flux: float32 [8, 128], P(None, 'freq'), may hold values from 0.5 to 2
- channel_ratio: float32 [128], P('freq'), may hold values from 0.7 to 1.4
- jones_gains: float32 [2, 8, 128, 512], P(None, None, 'freq'), may hold values from -4 to 4
- scaled_dual: float32 [2, 8, 128, 512], P(None, None, 'freq'), may hold values from -2 to 2
- consensus: float32 [2, 3, 8, 512], replicated, may hold values from -3 to 3
- penalty: float32 [8], replicated, may hold values from 0.3 to 3
Outputs:
- new_gains: float32 [2, 8, 128, 512], P(None, None, 'freq')
- new_consensus: float32 [2, 3, 8, 512], replicated
- new_dual: float32 [2, 8, 128, 512], P(None, None, 'freq')
- residuals: float32 [2, 2, 128, 8192], P(None, None, 'freq', 'bl')
Inputs may be any that keep to these rules, and one draw needn't show every extreme that they name: `baseline_station_pair`: the two stations of every baseline differ.
All inputs are finite; a program needn't handle non-finite values.
Results may differ from a plain program's by a relative error of at most 0.00016.
Values sent between devices are 32-bit elements; how exact they have to be, the bound alone decides.
A program may use at most 64 MiB of HBM per device.

v0:
```python
import math
import jax
import jax.numpy as jnp
from jax import lax
from jax.sharding import PartitionSpec as P

NPOLY = 3
ITERS = 3
robust_dof = 2.0
small_term = 1e-06
two_pi = 2.0 * math.pi


def legendre(ratios):
    scaled = (ratios - 1.05) / 0.35
    values = [jnp.ones_like(scaled), scaled]
    values.append((3 * scaled * values[1] - 1 * values[0]) / 2)
    return jnp.stack(values[:NPOLY])


def coherency(coords, sky_dirs, fluxes, ratios):
    project = (
        sky_dirs[0][:, None, None] * coords[0][None] + sky_dirs[1][:, None, None] * coords[1][None]
    )
    phases = two_pi * project[:, :, None, :] * ratios[None, None, :, None]
    amplitude = fluxes[:, None, :, None]
    return (amplitude * jnp.cos(phases), amplitude * jnp.sin(phases))


def station_table(pair_row, station_list):
    positions = lax.broadcasted_iota(jnp.int32, (station_list, pair_row.shape[0]), 0)
    return (positions == pair_row[None, :]).astype(jnp.float32)


def pick_stations(gain_re, gain_im, table):
    stacked = jnp.stack([gain_re, gain_im])
    lead_shape = stacked.shape[:3]
    flat = stacked.reshape(-1, stacked.shape[3])
    picked = jnp.dot(
        flat, table, precision=lax.Precision.HIGHEST, preferred_element_type=jnp.float32
    )
    picked = picked.reshape(lead_shape + (table.shape[1],))
    return (picked[0], picked[1])


def predict(gain_re, gain_im, left_table, right_table, sky_re, sky_im):
    left_re, left_im = pick_stations(gain_re, gain_im, left_table)
    right_re, right_im = pick_stations(gain_re, gain_im, right_table)
    pair_re = left_re * right_re + left_im * right_im
    pair_im = left_im * right_re - left_re * right_im
    model_re = pair_re[:, None] * sky_re - pair_im[:, None] * sky_im
    model_im = pair_re[:, None] * sky_im + pair_im[:, None] * sky_re
    return ((left_re, left_im, right_re, right_im), model_re, model_im)


def residual_of(observed, model_re, model_im):
    return (observed[0] - jnp.sum(model_re, axis=0), observed[1] - jnp.sum(model_im, axis=0))


def robust_weights(flagged, error_re, error_im, sigma_sq):
    return (
        flagged
        * (robust_dof + 1.0)
        / (robust_dof + (error_re * error_re + error_im * error_im) / sigma_sq)
    )


def normal_terms(
    error_re,
    error_im,
    model_re,
    model_im,
    weights,
    sky_re,
    sky_im,
    side_gains,
    left_table,
    right_table,
):
    target_re = error_re[None] + model_re
    target_im = error_im[None] + model_im
    cross_re = sky_re * target_re + sky_im * target_im
    cross_im = sky_re * target_im - sky_im * target_re
    weight_wide = weights[None]
    summed_re = jnp.sum(weight_wide * cross_re, axis=1)
    summed_im = jnp.sum(weight_wide * cross_im, axis=1)
    powers = jnp.sum(weight_wide * (sky_re * sky_re + sky_im * sky_im), axis=1)
    left_re, left_im, right_re, right_im = side_gains
    first_re = right_re * summed_re - right_im * summed_im
    first_im = right_re * summed_im + right_im * summed_re
    second_re = left_re * summed_re + left_im * summed_im
    second_im = left_im * summed_re - left_re * summed_im
    first_norm = (right_re * right_re + right_im * right_im) * powers
    second_norm = (left_re * left_re + left_im * left_im) * powers
    stacked_first = jnp.stack([first_re, first_im, first_norm])
    stacked_second = jnp.stack([second_re, second_im, second_norm])
    lead_shape = stacked_first.shape[:3]
    baseline_count = stacked_first.shape[3]
    contract = (((1,), (1,)), ((), ()))
    into_first = lax.dot_general(
        stacked_first.reshape(-1, baseline_count),
        left_table,
        contract,
        precision=lax.Precision.HIGHEST,
        preferred_element_type=jnp.float32,
    )
    into_second = lax.dot_general(
        stacked_second.reshape(-1, baseline_count),
        right_table,
        contract,
        precision=lax.Precision.HIGHEST,
        preferred_element_type=jnp.float32,
    )
    return (into_first + into_second).reshape(lead_shape + (left_table.shape[0],))


def update_gains(gain_re, gain_im, normal_sums, anchor_re, anchor_im, effective_penalty):
    penalty_wide = effective_penalty[:, None, None]
    divisor = normal_sums[2] + penalty_wide
    solved_re = (normal_sums[0] + penalty_wide * anchor_re) / divisor
    solved_im = (normal_sums[1] + penalty_wide * anchor_im) / divisor
    return (0.5 * (gain_re + solved_re), 0.5 * (gain_im + solved_im))


def cholesky_solve(gram_total, flat_rhs):
    factor = jnp.linalg.cholesky(gram_total)
    matrix_order = gram_total.shape[0]
    forward = []
    for row_index in range(matrix_order):
        running = flat_rhs[row_index]
        for col_index in range(row_index):
            running = running - factor[row_index, col_index] * forward[col_index]
        forward.append(running / factor[row_index, row_index])
    backward = [None] * matrix_order
    for row_index in reversed(range(matrix_order)):
        running = forward[row_index]
        for col_index in range(row_index + 1, matrix_order):
            running = running - factor[col_index, row_index] * backward[col_index]
        backward[row_index] = running / factor[row_index, row_index]
    return jnp.stack(backward)


def solve_consensus(gram_total, rhs_total):
    matrix_order = gram_total.shape[0]
    flat_rhs = jnp.moveaxis(rhs_total, 1, 0).reshape(matrix_order, -1)
    solved = cholesky_solve(gram_total, flat_rhs)
    return jnp.moveaxis(
        solved.reshape((matrix_order, rhs_total.shape[0]) + rhs_total.shape[2:]), 0, 1
    )


def body(
    visibilities,
    sample_flag_weight,
    baseline_station_pair,
    baseline_spatial_coords,
    directions,
    source_flux,
    channel_ratio,
    jones_gains,
    scaled_dual,
    consensus,
    penalty,
):
    station_list = jones_gains.shape[3]
    baseline_list = baseline_station_pair.shape[1] * lax.axis_size("bl")
    solution_time_slots = visibilities.shape[1]
    effective_penalty = penalty * (2.0 * baseline_list * solution_time_slots / station_list)
    left_table = station_table(baseline_station_pair[0], station_list)
    right_table = station_table(baseline_station_pair[1], station_list)
    sky_re, sky_im = coherency(baseline_spatial_coords, directions, source_flux, channel_ratio)
    poly_basis = legendre(channel_ratio)
    gram_local = jnp.dot(poly_basis, poly_basis.T, precision=lax.Precision.HIGHEST)
    anchor = (
        jnp.einsum("jc,xjks->xkcs", poly_basis, consensus, precision=lax.Precision.HIGHEST)
        - scaled_dual
    )
    anchor_re, anchor_im = (anchor[0], anchor[1])
    flagged = sample_flag_weight.astype(jnp.float32)
    count_local = jnp.sum(flagged)
    gain_re, gain_im = (jones_gains[0], jones_gains[1])
    for iteration in range(ITERS):
        side_gains, model_re, model_im = predict(
            gain_re, gain_im, left_table, right_table, sky_re, sky_im
        )
        error_re, error_im = residual_of(visibilities, model_re, model_im)
        misfit_local = jnp.sum(flagged * (error_re * error_re + error_im * error_im))
        squares, weight_total = lax.psum((misfit_local, count_local), ("bl", "freq"))
        sigma_sq = squares / (weight_total + 1.0) + small_term
        weights = robust_weights(flagged, error_re, error_im, sigma_sq)
        partial_value = normal_terms(
            error_re,
            error_im,
            model_re,
            model_im,
            weights,
            sky_re,
            sky_im,
            side_gains,
            left_table,
            right_table,
        )
        owned_sums = lax.psum_scatter(partial_value, "bl", scatter_dimension=3, tiled=True)
        own_width = owned_sums.shape[3]
        offset = lax.axis_index("bl") * own_width
        own_gain_re = lax.dynamic_slice_in_dim(gain_re, offset, own_width, 2)
        own_gain_im = lax.dynamic_slice_in_dim(gain_im, offset, own_width, 2)
        own_anchor_re = lax.dynamic_slice_in_dim(anchor_re, offset, own_width, 2)
        own_anchor_im = lax.dynamic_slice_in_dim(anchor_im, offset, own_width, 2)
        new_re, new_im = update_gains(
            own_gain_re, own_gain_im, owned_sums, own_anchor_re, own_anchor_im, effective_penalty
        )
        gathered = lax.all_gather(jnp.stack([new_re, new_im]), "bl", axis=3, tiled=True)
        gain_re, gain_im = (gathered[0], gathered[1])
    side_gains, model_re, model_im = predict(
        gain_re, gain_im, left_table, right_table, sky_re, sky_im
    )
    error_re, error_im = residual_of(visibilities, model_re, model_im)
    residuals = jnp.stack([error_re, error_im])
    new_gains = jnp.stack([gain_re, gain_im])
    rhs_local = jnp.einsum(
        "jc,xkcs->xjks", poly_basis, new_gains + scaled_dual, precision=lax.Precision.HIGHEST
    )
    rhs_total, gram_total = lax.psum((rhs_local, gram_local), "freq")
    new_consensus = solve_consensus(gram_total, rhs_total)
    new_dual = (
        scaled_dual
        + new_gains
        - jnp.einsum("jc,xjks->xkcs", poly_basis, new_consensus, precision=lax.Precision.HIGHEST)
    )
    return (new_gains, new_consensus, new_dual, residuals)


def solution(mesh):
    in_specs = (
        P(None, None, "freq", "bl"),
        P(None, "freq", "bl"),
        P(None, "bl"),
        P(None, None, "bl"),
        P(),
        P(None, "freq"),
        P("freq"),
        P(None, None, "freq", None),
        P(None, None, "freq", None),
        P(),
        P(),
    )
    out_specs = (
        P(None, None, "freq", None),
        P(),
        P(None, None, "freq", None),
        P(None, None, "freq", "bl"),
    )
    return jax.shard_map(body, mesh=mesh, in_specs=in_specs, out_specs=out_specs, check_vma=False)
```

profile of v0, /device:TPU:8, one launch (start us, length us, event | category | flops | bytes accessed | tf_op | source)
XLA Modules:
  0.0 447.2 jit_solution(5179471884949867166)
XLA Ops:
  8.1 3.2 fusion.14
  13.5 2.4 multiply_add_fusion.3
  16.0 9.0 %fusion.102 = (f32[2,16,2048]{2,1,0:T(8,128)S(1)}, f32[2,16,2048]{2,1,0:T(8,128)S(1)}) fusion(f32[8,16,2048]{2,1,0:T(8,128)S(1)} %bitcast.263, f32[16]{0:T(128)S(1)} %copy-done.28, f32[8,2,2048]{2,1,0:T(2,128)S(1)} %add_multiply_fusion, f32[8,16]{1,0:T(8,128)S(1)} %copy-done.26, f32[8,16,2048]{2,1,0:T(8,128)S(1)} %bitcast.261), kind=kLoop, calls=%fused_computation.115 | loop fusion | flops 5636096 | bytes 2753088 | tf_op jit(solution)/shard_map/reduce_sum | solution.py:57
  27.2 40.9 %all-reduce = (f32[]{:T(128)}, f32[]{:T(128)}) all-reduce(f32[]{:T(128)} %get-tuple-element.34, f32[]{:T(128)} %get-tuple-element.33), channel_id=1, replica_groups=mesh['bl'=4,'freq'=8] {'bl','freq'}, use_global_device_ids=true, to_apply=%region_3.0 | all-reduce | flops 2 | bytes 16 | tf_op jit(solution)/shard_map/psum | solution.py:188
  70.4 10.9 %fusion.36 = (f32[8,16,2048]{2,1,0:T(8,128)S(1)}, f32[8,16,2048]{2,1,0:T(8,128)S(1)}, f32[8,16,2048]{2,1,0:T(8,128)S(1)}) fusion(f32[2,16,2048]{2,1,0:T(8,128)} %get-tuple-element.104, f32[2,16,2048]{2,1,0:T(8,128)S(1)} %get-tuple-element.103, f32[2,16,2048]{2,1,0:T(8,128)S(1)} %add_divide_fusion.2, f32[8,16,2048]{2,1,0:T(8,128)S(1)} %bitcast.264, ...), kind=kLoop, calls=%fused_computation.46 | loop fusion | flops 12845056 | bytes 6160960 | tf_op jit(solution)/shard_map/reduce_sum | solution.py:85
  83.7 3.0 fusion.5
  86.7 3.9 fusion.103
  92.5 24.4 %reduce-scatter.4.cloned.1.call-done = f32[3,8,16,128]{3,2,1,0:T(8,128)} async-done(((f32[3,8,16,512]{3,2,1,0:T(8,128)}), f32[3,8,16,128]{3,2,1,0:T(8,128)}) %reduce-scatter.4.cloned.1.call-update) | async-done | bytes 196624 | tf_op jit(solution)/shard_map/reduce_scatter | solution.py:203
  118.0 13.3 %all_gather.9 = f32[2,8,16,512]{3,2,1,0:T(8,128)S(1)} all-gather(f32[2,8,16,128]{3,2,1,0:T(8,128)S(1)} %pad_maximum_fusion.7), channel_id=1, replica_groups=mesh['bl'=4,'freq'=8] {'bl'}, dimensions={3}, use_global_device_ids=true | all-gather | bytes 655360 | tf_op jit(solution)/shard_map/all_gather | solution.py:213
  135.5 2.4 multiply_add_fusion.2
  137.9 9.0 %fusion.98 = (f32[2,16,2048]{2,1,0:T(8,128)S(1)}, f32[2,16,2048]{2,1,0:T(8,128)S(1)}) fusion(f32[8,16,2048]{2,1,0:T(8,128)S(1)} %bitcast.271, f32[8,16,2048]{2,1,0:T(8,128)S(1)} %bitcast.269, f32[16]{0:T(128)S(1)} %copy-done.28, f32[8,2,2048]{2,1,0:T(2,128)S(1)} %add_multiply_fusion, f32[8,16]{1,0:T(8,128)S(1)} %copy-done.26), kind=kLoop, calls=%fused_computation.111 | loop fusion | flops 5636096 | bytes 2753088 | tf_op jit(solution)/shard_map/reduce_sum | solution.py:57
  149.1 39.8 %psum.50 = f32[]{:T(128)} all-reduce(f32[]{:T(128)} %get-tuple-element.42), channel_id=1, replica_groups=mesh['bl'=4,'freq'=8] {'bl','freq'}, use_global_device_ids=true, to_apply=%region_13.0 | all-reduce | flops 1 | bytes 8 | tf_op jit(solution)/shard_map/psum | solution.py:188
  190.5 10.9 %fusion.45 = (f32[8,16,2048]{2,1,0:T(8,128)S(1)}, f32[8,16,2048]{2,1,0:T(8,128)S(1)}, f32[8,16,2048]{2,1,0:T(8,128)S(1)}) fusion(f32[2,16,2048]{2,1,0:T(8,128)} %get-tuple-element.98, f32[2,16,2048]{2,1,0:T(8,128)S(1)} %get-tuple-element.97, f32[2,16,2048]{2,1,0:T(8,128)S(1)} %add_divide_fusion.1, f32[8,16,2048]{2,1,0:T(8,128)S(1)} %bitcast.272, ...), kind=kLoop, calls=%fused_computation.55 | loop fusion | flops 12845056 | bytes 6160960 | tf_op jit(solution)/shard_map/reduce_sum | solution.py:85
  203.2 3.0 fusion.3
  206.6 3.9 fusion.104
  210.6 26.2 %reduce-scatter.6.cloned.1.call-done = f32[3,8,16,128]{3,2,1,0:T(8,128)} async-done(((f32[3,8,16,512]{3,2,1,0:T(8,128)}), f32[3,8,16,128]{3,2,1,0:T(8,128)}) %reduce-scatter.6.cloned.1.call-update) | async-done | bytes 196624 | tf_op jit(solution)/shard_map/reduce_scatter | solution.py:203
  237.9 13.5 %all_gather.10 = f32[2,8,16,512]{3,2,1,0:T(8,128)S(1)} all-gather(f32[2,8,16,128]{3,2,1,0:T(8,128)S(1)} %pad_maximum_fusion.8), channel_id=1, replica_groups=mesh['bl'=4,'freq'=8] {'bl'}, dimensions={3}, use_global_device_ids=true | all-gather | bytes 655360 | tf_op jit(solution)/shard_map/all_gather | solution.py:213
  255.7 2.4 multiply_add_fusion.1
  258.0 9.0 %fusion.94 = (f32[2,16,2048]{2,1,0:T(8,128)S(1)}, f32[2,16,2048]{2,1,0:T(8,128)S(1)}) fusion(f32[8,16,2048]{2,1,0:T(8,128)S(1)} %bitcast.267, f32[8,16,2048]{2,1,0:T(8,128)S(1)} %bitcast.265, f32[16]{0:T(128)S(1)} %copy-done.28, f32[8,2,2048]{2,1,0:T(2,128)S(1)} %add_multiply_fusion, f32[8,16]{1,0:T(8,128)S(1)} %copy-done.26), kind=kLoop, calls=%fused_computation.107 | loop fusion | flops 5636096 | bytes 2753088 | tf_op jit(solution)/shard_map/reduce_sum | solution.py:57
  269.2 39.7 %psum.51 = f32[]{:T(128)} all-reduce(f32[]{:T(128)} %get-tuple-element.40), channel_id=1, replica_groups=mesh['bl'=4,'freq'=8] {'bl','freq'}, use_global_device_ids=true, to_apply=%region_21.0 | all-reduce | flops 1 | bytes 8 | tf_op jit(solution)/shard_map/psum | solution.py:188
  310.6 10.9 %fusion.53 = (f32[8,16,2048]{2,1,0:T(8,128)S(1)}, f32[8,16,2048]{2,1,0:T(8,128)S(1)}, f32[8,16,2048]{2,1,0:T(8,128)S(1)}) fusion(f32[2,16,2048]{2,1,0:T(8,128)} %get-tuple-element.94, f32[2,16,2048]{2,1,0:T(8,128)S(1)} %get-tuple-element.93, f32[2,16,2048]{2,1,0:T(8,128)S(1)} %add_divide_fusion, f32[8,16,2048]{2,1,0:T(8,128)S(1)} %bitcast.268, ...), kind=kLoop, calls=%fused_computation.63 | loop fusion | flops 12845056 | bytes 6160960 | tf_op jit(solution)/shard_map/reduce_sum | solution.py:85
  323.3 3.0 fusion.1
  326.7 3.9 fusion.105
  330.9 11.1 %psum.53 = f32[3,3]{0,1:T(4,128)S(1)} all-reduce(f32[3,3]{0,1:T(4,128)S(1)} %fusion.163), channel_id=1, replica_groups=mesh['bl'=4,'freq'=8] {'freq'}, use_global_device_ids=true, to_apply=%region_27.0 | all-reduce | flops 9 | bytes 72 | tf_op jit(solution)/shard_map/psum | solution.py:224
  345.7 11.2 %reduce-scatter.8.cloned.1.call-done = f32[3,8,16,128]{3,2,1,0:T(8,128)} async-done(((f32[3,8,16,512]{3,2,1,0:T(8,128)}), f32[3,8,16,128]{3,2,1,0:T(8,128)}) %reduce-scatter.8.cloned.1.call-update) | async-done | bytes 196624 | tf_op jit(solution)/shard_map/reduce_scatter | solution.py:203
  358.0 13.3 %all_gather.11 = f32[2,8,16,512]{3,2,1,0:T(8,128)S(1)} all-gather(f32[2,8,16,128]{3,2,1,0:T(8,128)S(1)} %pad_maximum_fusion.9), channel_id=1, replica_groups=mesh['bl'=4,'freq'=8] {'bl'}, dimensions={3}, use_global_device_ids=true | all-gather | bytes 655360 | tf_op jit(solution)/shard_map/all_gather | solution.py:213
  371.3 3.4 fusion
  374.7 3.4 fusion.7
  379.4 2.5 multiply_add_fusion
  381.9 8.9 %fusion.58 = (f32[2,16,2048]{2,1,0:T(8,128)S(1)}, f32[2,16,2048]{2,1,0:T(8,128)S(1)}) fusion(f32[8,16,2048]{2,1,0:T(8,128)S(1)} %bitcast.276, f32[8,16,2048]{2,1,0:T(8,128)S(1)} %bitcast.275, f32[16]{0:T(128)S(1)} %copy-done.28, f32[8,2,2048]{2,1,0:T(2,128)S(1)} %add_multiply_fusion, f32[8,16]{1,0:T(8,128)S(1)} %copy-done.26), kind=kLoop, calls=%fused_computation.68 | loop fusion | flops 5636096 | bytes 2753088 | tf_op jit(solution)/shard_map/reduce_sum | solution.py:57
  391.7 41.8 %all-reduce.3.cloned.1.call-done = f32[3,2,8,512]{3,2,1,0:T(8,128)} async-done(((f32[3,2,8,512]{3,2,1,0:T(8,128)}), f32[3,2,8,512]{3,2,1,0:T(8,128)}) %all-reduce.3.cloned.1.call-update) | async-done | bytes 98320 | tf_op jit(solution)/shard_map/psum | solution.py:224
  433.5 4.0 subtract_divide_fusion
  (127 shorter events, 40.5 us)
Async XLA Ops:
  7.2 83.7 %copy-start = (f32[2,3,8,512]{3,2,1,0:T(8,128)S(1)}, f32[2,3,8,512]{3,2,1,0:T(8,128)}, u32[]{:S(2)}) copy-start(f32[2,3,8,512]{3,2,1,0:T(8,128)} %param.20) | copy-start | bytes 294916
  7.2 109.8 %reduce-scatter.4.cloned.1.call-start = ((), (), s32[]{:S(2)}) async-start(), calls=%async_computation.3 | async-start | bytes 983040 | tf_op jit(solution)/shard_map/reduce_scatter | solution.py:203
  8.0 3.2 copy-start.24
  11.3 2.1 copy-start.29
  13.4 2.6 copy-start.26
  13.5 2.5 copy-start.28
  15.8 9.2 %copy-start.2 = (f32[2,2,16,2048]{3,2,1,0:T(8,128)S(1)}, f32[2,2,16,2048]{3,2,1,0:T(8,128)}, u32[]{:S(2)}) copy-start(f32[2,2,16,2048]{3,2,1,0:T(8,128)} %param.11) | copy-start | bytes 1572868
  16.0 9.8 %copy-start.3 = (s32[2,16,2048]{2,1,0:T(8,128)S(1)}, s32[2,16,2048]{2,1,0:T(8,128)}, u32[]{:S(2)}) copy-start(s32[2,16,2048]{2,1,0:T(8,128)} %param.12) | copy-start | bytes 786436
  70.4 10.9 %copy-start.4 = (f32[128,2048]{1,0:T(8,128)S(1)}, f32[128,2048]{1,0:T(8,128)}, u32[]{:S(2)}) copy-start(f32[128,2048]{1,0:T(8,128)} %get-tuple-element.85) | copy-start | bytes 3145732
  70.4 10.9 %copy-start.5 = (f32[128,2048]{1,0:T(8,128)S(1)}, f32[128,2048]{1,0:T(8,128)}, u32[]{:S(2)}) copy-start(f32[128,2048]{1,0:T(8,128)} %get-tuple-element.86) | copy-start | bytes 3145732
  70.4 10.9 %copy-start.6 = (f32[128,2048]{1,0:T(8,128)S(1)}, f32[128,2048]{1,0:T(8,128)}, u32[]{:S(2)}) copy-start(f32[128,2048]{1,0:T(8,128)} %get-tuple-element.87) | copy-start | bytes 3145732
  70.4 10.9 %copy-start.7 = (f32[128,2048]{1,0:T(8,128)S(1)}, f32[128,2048]{1,0:T(8,128)}, u32[]{:S(2)}) copy-start(f32[128,2048]{1,0:T(8,128)} %get-tuple-element.88) | copy-start | bytes 3145732
  86.7 4.0 copy-start.30
  86.7 4.1 copy-start.25
  90.7 146.1 %reduce-scatter.6.cloned.1.call-start = ((), (), s32[]{:S(2)}) async-start(), calls=%async_computation.4 | async-start | bytes 983040 | tf_op jit(solution)/shard_map/reduce_scatter | solution.py:203
  92.5 40.8 %copy-start.22 = (f32[1,8,16,512]{3,2,1,0:T(8,128)}, f32[1,8,16,512]{3,2,1,0:T(8,128)S(1)}, u32[]{:S(2)}) copy-start(f32[1,8,16,512]{3,2,1,0:T(8,128)S(1)} %get-tuple-element.99) | copy-start | bytes 786436
  92.5 40.8 %copy-start.23 = (f32[1,8,16,512]{3,2,1,0:T(8,128)}, f32[1,8,16,512]{3,2,1,0:T(8,128)S(1)}, u32[]{:S(2)}) copy-start(f32[1,8,16,512]{3,2,1,0:T(8,128)S(1)} %get-tuple-element.100) | copy-start | bytes 786436
  131.2 2.1 copy-start.20
  190.5 10.9 %copy-start.12 = (f32[128,2048]{1,0:T(8,128)S(1)}, f32[128,2048]{1,0:T(8,128)}, u32[]{:S(2)}) copy-start(f32[128,2048]{1,0:T(8,128)} %get-tuple-element.77) | copy-start | bytes 3145732
  190.5 10.9 %copy-start.13 = (f32[128,2048]{1,0:T(8,128)S(1)}, f32[128,2048]{1,0:T(8,128)}, u32[]{:S(2)}) copy-start(f32[128,2048]{1,0:T(8,128)} %get-tuple-element.78) | copy-start | bytes 3145732
  190.5 10.9 %copy-start.14 = (f32[128,2048]{1,0:T(8,128)S(1)}, f32[128,2048]{1,0:T(8,128)}, u32[]{:S(2)}) copy-start(f32[128,2048]{1,0:T(8,128)} %get-tuple-element.79) | copy-start | bytes 3145732
  190.5 10.9 %copy-start.15 = (f32[128,2048]{1,0:T(8,128)S(1)}, f32[128,2048]{1,0:T(8,128)}, u32[]{:S(2)}) copy-start(f32[128,2048]{1,0:T(8,128)} %get-tuple-element.80) | copy-start | bytes 3145732
  206.6 4.0 copy-start.21
  210.5 146.4 %reduce-scatter.8.cloned.1.call-start = ((), (), s32[]{:S(2)}) async-start(), calls=%async_computation.5 | async-start | bytes 983040 | tf_op jit(solution)/shard_map/reduce_scatter | solution.py:203
  310.6 10.9 %copy-start.8 = (f32[128,2048]{1,0:T(8,128)S(1)}, f32[128,2048]{1,0:T(8,128)}, u32[]{:S(2)}) copy-start(f32[128,2048]{1,0:T(8,128)} %get-tuple-element.69) | copy-start | bytes 3145732
  310.6 10.9 %copy-start.9 = (f32[128,2048]{1,0:T(8,128)S(1)}, f32[128,2048]{1,0:T(8,128)}, u32[]{:S(2)}) copy-start(f32[128,2048]{1,0:T(8,128)} %get-tuple-element.70) | copy-start | bytes 3145732
  310.6 10.9 %copy-start.10 = (f32[128,2048]{1,0:T(8,128)S(1)}, f32[128,2048]{1,0:T(8,128)}, u32[]{:S(2)}) copy-start(f32[128,2048]{1,0:T(8,128)} %get-tuple-element.71) | copy-start | bytes 3145732
  310.6 10.9 %copy-start.11 = (f32[128,2048]{1,0:T(8,128)S(1)}, f32[128,2048]{1,0:T(8,128)}, u32[]{:S(2)}) copy-start(f32[128,2048]{1,0:T(8,128)} %get-tuple-element.72) | copy-start | bytes 3145732
  326.7 19.0 %copy-start.19 = (f32[2,8,16,512]{3,2,1,0:T(8,128)S(1)}, f32[2,8,16,512]{3,2,1,0:T(8,128)}, u32[]{:S(2)}) copy-start(f32[2,8,16,512]{3,2,1,0:T(8,128)} %copy-done.18) | copy-start | bytes 1572868
  330.6 102.9 %all-reduce.3.cloned.1.call-start = ((), (), s32[]{:S(2)}) async-start(), calls=%async_computation.6 | async-start | bytes 196608 | tf_op jit(solution)/shard_map/psum | solution.py:224
  374.7 3.5 copy-start.17
  390.8 49.6 %copy-start.1 = (f32[2,3,8,512]{3,2,1,0:T(8,128)S(1)}, f32[2,3,8,512]{3,2,1,0:T(8,128)}, u32[]{:S(2)}) copy-start(f32[2,3,8,512]{3,2,1,0:T(8,128)} %param.20) | copy-start | bytes 294916
  (3 other events, 5.3 us)
Sparse Core Ops, SparseCore 0:
  90.8 26.0 reduce-scatter.3
  210.7 26.1 reduce-scatter.5
  330.7 26.1 reduce-scatter.7
  379.5 54.0 all-reduce.2
where the time goes:
time: 453 us; the launch traced here: 447 us
  blocking collectives  171 us (38%)
  other arithmetic  104 us (23%)
  waiting for transfers between devices  104 us (23%)
  matrix products  44.3 us (10%)
  between operations  18.7 us (4%)
  local copies, waits for them, and re-layouts  4.85 us (1%)
    psum x3, blocking collectives, body(): lax.psum((misfit_local, count_local), ('bl', 'freq'))  120 us
    reduce_scatter x3, waiting for transfers between devices, body(): lax.psum_scatter(partial_value, 'bl', scatter_dimension=3, tiled=True)  61.8 us
    psum x1, waiting for transfers between devices, body(): rhs_total, gram_total = lax.psum((rhs_local, gram_local), 'freq')  41.8 us
    all_gather x3, blocking collectives, body(): lax.all_gather(jnp.stack([new_re, new_im]), 'bl', axis=3, tiled=True)  40 us
    reduce_sum x4, other arithmetic, residual_of(): jnp.sum(model_re, axis=0)  35.9 us
    reduce_sum x3, other arithmetic, normal_terms(): summed_re = jnp.sum(weight_wide * cross_re, axis=1)  32.6 us
    dot_general x8, matrix products, pick_stations(): jnp.dot(flat, table, precision=lax.Precision.HIGHEST, preferred_element_t...  20.6 us
    dot_general x3, matrix products, normal_terms(): lax.dot_general(stacked_second.reshape(-1, baseline_count), right_table,...  11.8 us
  transfers between devices with their start and end apart: 4, of which 4 were waited for; matrix products, arithmetic and copies ran while one was open for 4% of the time, Pallas kernels for 0%

commit v1 on v0

--- a/solution.py
+++ b/solution.py
@@ -9,6 +9,7 @@
 robust_dof = 2.0
 small_term = 1e-06
 two_pi = 2.0 * math.pi
+remake_the_roads = lambda local_x, ax_name, axis_key: lax.psum(lax.psum(local_x, ax_name), axis_key)
 
 
 def legendre(ratios):
@@ -185,7 +186,7 @@
         )
         error_re, error_im = residual_of(visibilities, model_re, model_im)
         misfit_local = jnp.sum(flagged * (error_re * error_re + error_im * error_im))
-        squares, weight_total = lax.psum((misfit_local, count_local), ("bl", "freq"))
+        squares, weight_total = remake_the_roads((misfit_local, count_local), "bl", "freq")
         sigma_sq = squares / (weight_total + 1.0) + small_term
         weights = robust_weights(flagged, error_re, error_im, sigma_sq)
         partial_value = normal_terms(

time: 453 us -> 399 us (0.88)
  blocking collectives: 171 us -> 103 us
  waiting for transfers between devices: 104 us -> 115 us
    psum x4 -> x6, blocking collectives: 131 us -> 63.2 us  [the longest x3 33.6 us: lax.psum(lax.psum(local_x, ax_name), axis_key)]
    reduce_scatter x3, waiting for transfers between devices: 61.8 us -> 73.4 us  [body(): lax.psum_scatter(partial_value, 'bl', scatter_dimension=3, tiled=True)]
where the time goes in v1:
time: 399 us; the launch traced here: 393 us
  waiting for transfers between devices  115 us (29%)
  other arithmetic  106 us (27%)
  blocking collectives  103 us (26%)
  matrix products  44.3 us (11%)
  between operations  18.7 us (5%)
  local copies, waits for them, and re-layouts  5.56 us (1%)
    reduce_scatter x3, waiting for transfers between devices, body(): lax.psum_scatter(partial_value, 'bl', scatter_dimension=3, tiled=True)  73.4 us
    psum x1, waiting for transfers between devices, body(): rhs_total, gram_total = lax.psum((rhs_local, gram_local), 'freq')  41.7 us
    all_gather x3, blocking collectives, body(): lax.all_gather(jnp.stack([new_re, new_im]), 'bl', axis=3, tiled=True)  40 us
    reduce_sum x4, other arithmetic, residual_of(): jnp.sum(model_re, axis=0)  35.8 us
    psum x3, blocking collectives, lax.psum(lax.psum(local_x, ax_name), axis_key)  33.6 us
    reduce_sum x3, other arithmetic, normal_terms(): summed_re = jnp.sum(weight_wide * cross_re, axis=1)  32.7 us
    psum x3, blocking collectives, lax.psum(local_x, ax_name)  29.6 us
    dot_general x8, matrix products, pick_stations(): jnp.dot(flat, table, precision=lax.Precision.HIGHEST, preferred_element_t...  20.6 us
  transfers between devices with their start and end apart: 4, of which 4 were waited for; matrix products, arithmetic and copies ran while one was open for 4% of the time, Pallas kernels for 0%

profile of v1, /device:TPU:8, one launch (start us, length us, event | category | flops | bytes accessed | tf_op | source)
XLA Modules:
  0.0 393.0 jit_solution(8092292597566114061)
XLA Ops:
  8.1 3.2 fusion.14
  13.5 2.4 multiply_add_fusion.3
  16.0 9.0 %fusion.102 = (f32[2,16,2048]{2,1,0:T(8,128)S(1)}, f32[2,16,2048]{2,1,0:T(8,128)S(1)}) fusion(f32[8,16,2048]{2,1,0:T(8,128)S(1)} %bitcast.263, f32[16]{0:T(128)S(1)} %copy-done.30, f32[8,2,2048]{2,1,0:T(2,128)S(1)} %add_multiply_fusion, f32[8,16]{1,0:T(8,128)S(1)} %copy-done.28, f32[8,16,2048]{2,1,0:T(8,128)S(1)} %bitcast.261), kind=kLoop, calls=%fused_computation.115 | loop fusion | flops 5636096 | bytes 2753088 | tf_op jit(solution)/shard_map/reduce_sum | solution.py:58
  27.2 10.5 %all-reduce.2 = (f32[]{:T(128)}, f32[]{:T(128)}) all-reduce(f32[]{:T(128)} %get-tuple-element.34, f32[]{:T(128)} %get-tuple-element.33), channel_id=1, replica_groups=mesh['bl'=4,'freq'=8] {'bl'}, use_global_device_ids=true, to_apply=%region_3.0 | all-reduce | flops 2 | bytes 16 | tf_op jit(solution)/shard_map/psum | solution.py:12
  37.7 11.8 %all-reduce.1 = (f32[]{:T(128)}, f32[]{:T(128)}) all-reduce(f32[]{:T(128)} %get-tuple-element.39, f32[]{:T(128)} %get-tuple-element.40), channel_id=1, replica_groups=mesh['bl'=4,'freq'=8] {'freq'}, use_global_device_ids=true, to_apply=%region_4.0 | all-reduce | flops 2 | bytes 16 | tf_op jit(solution)/shard_map/psum | solution.py:12
  51.9 10.9 %fusion.36 = (f32[8,16,2048]{2,1,0:T(8,128)S(1)}, f32[8,16,2048]{2,1,0:T(8,128)S(1)}, f32[8,16,2048]{2,1,0:T(8,128)S(1)}) fusion(f32[2,16,2048]{2,1,0:T(8,128)} %get-tuple-element.108, f32[2,16,2048]{2,1,0:T(8,128)S(1)} %get-tuple-element.107, f32[2,16,2048]{2,1,0:T(8,128)S(1)} %add_divide_fusion.2, f32[8,16,2048]{2,1,0:T(8,128)S(1)} %bitcast.264, ...), kind=kLoop, calls=%fused_computation.46 | loop fusion | flops 12845056 | bytes 6160960 | tf_op jit(solution)/shard_map/reduce_sum | solution.py:86
  65.1 3.0 fusion.5
  68.2 3.9 fusion.103
  73.3 25.2 %reduce-scatter.4.cloned.1.call-done = f32[3,8,16,128]{3,2,1,0:T(8,128)} async-done(((f32[3,8,16,512]{3,2,1,0:T(8,128)}), f32[3,8,16,128]{3,2,1,0:T(8,128)}) %reduce-scatter.4.cloned.1.call-update) | async-done | bytes 196624 | tf_op jit(solution)/shard_map/reduce_scatter | solution.py:204
  99.5 13.2 %all_gather.9 = f32[2,8,16,512]{3,2,1,0:T(8,128)S(1)} all-gather(f32[2,8,16,128]{3,2,1,0:T(8,128)S(1)} %pad_maximum_fusion.7), channel_id=1, replica_groups=mesh['bl'=4,'freq'=8] {'bl'}, dimensions={3}, use_global_device_ids=true | all-gather | bytes 655360 | tf_op jit(solution)/shard_map/all_gather | solution.py:214
  119.4 8.9 %fusion.98 = (f32[2,16,2048]{2,1,0:T(8,128)S(1)}, f32[2,16,2048]{2,1,0:T(8,128)S(1)}) fusion(f32[8,16,2048]{2,1,0:T(8,128)S(1)} %bitcast.271, f32[8,16,2048]{2,1,0:T(8,128)S(1)} %bitcast.269, f32[16]{0:T(128)S(1)} %copy-done.30, f32[8,2,2048]{2,1,0:T(2,128)S(1)} %add_multiply_fusion, f32[8,16]{1,0:T(8,128)S(1)} %copy-done.28), kind=kLoop, calls=%fused_computation.111 | loop fusion | flops 5636096 | bytes 2753088 | tf_op jit(solution)/shard_map/reduce_sum | solution.py:58
  130.4 9.5 %psum.86 = f32[]{:T(128)} all-reduce(f32[]{:T(128)} %get-tuple-element.46), channel_id=1, replica_groups=mesh['bl'=4,'freq'=8] {'bl'}, use_global_device_ids=true, to_apply=%region_15.0 | all-reduce | flops 1 | bytes 8 | tf_op jit(solution)/shard_map/psum | solution.py:12
  141.7 11.0 %psum.87 = f32[]{:T(128)} all-reduce(f32[]{:T(128)} %psum.86), channel_id=1, replica_groups=mesh['bl'=4,'freq'=8] {'freq'}, use_global_device_ids=true, to_apply=%region_16.0 | all-reduce | flops 1 | bytes 8 | tf_op jit(solution)/shard_map/psum | solution.py:12
  154.4 10.9 %fusion.45 = (f32[8,16,2048]{2,1,0:T(8,128)S(1)}, f32[8,16,2048]{2,1,0:T(8,128)S(1)}, f32[8,16,2048]{2,1,0:T(8,128)S(1)}) fusion(f32[2,16,2048]{2,1,0:T(8,128)} %get-tuple-element.102, f32[2,16,2048]{2,1,0:T(8,128)} %get-tuple-element.101, f32[2,16,2048]{2,1,0:T(8,128)S(1)} %add_divide_fusion.1, f32[8,16,2048]{2,1,0:T(8,128)S(1)} %bitcast.272, ...), kind=kLoop, calls=%fused_computation.55 | loop fusion | flops 12845056 | bytes 6160960 | tf_op jit(solution)/shard_map/reduce_sum | solution.py:86
  167.2 3.0 fusion.3
  170.4 3.9 fusion.104
  174.7 25.8 %reduce-scatter.6.cloned.1.call-done = f32[3,8,16,128]{3,2,1,0:T(8,128)} async-done(((f32[3,8,16,512]{3,2,1,0:T(8,128)}), f32[3,8,16,128]{3,2,1,0:T(8,128)}) %reduce-scatter.6.cloned.1.call-update) | async-done | bytes 196624 | tf_op jit(solution)/shard_map/reduce_scatter | solution.py:204
  201.6 13.5 %all_gather.10 = f32[2,8,16,512]{3,2,1,0:T(8,128)S(1)} all-gather(f32[2,8,16,128]{3,2,1,0:T(8,128)S(1)} %pad_maximum_fusion.8), channel_id=1, replica_groups=mesh['bl'=4,'freq'=8] {'bl'}, dimensions={3}, use_global_device_ids=true | all-gather | bytes 655360 | tf_op jit(solution)/shard_map/all_gather | solution.py:214
  221.7 8.9 %fusion.94 = (f32[2,16,2048]{2,1,0:T(8,128)S(1)}, f32[2,16,2048]{2,1,0:T(8,128)S(1)}) fusion(f32[8,16,2048]{2,1,0:T(8,128)S(1)} %bitcast.267, f32[8,16,2048]{2,1,0:T(8,128)S(1)} %bitcast.265, f32[16]{0:T(128)S(1)} %copy-done.30, f32[8,2,2048]{2,1,0:T(2,128)S(1)} %add_multiply_fusion, f32[8,16]{1,0:T(8,128)S(1)} %copy-done.28), kind=kLoop, calls=%fused_computation.107 | loop fusion | flops 5636096 | bytes 2753088 | tf_op jit(solution)/shard_map/reduce_sum | solution.py:58
  232.8 9.5 %psum.88 = f32[]{:T(128)} all-reduce(f32[]{:T(128)} %get-tuple-element.44), channel_id=1, replica_groups=mesh['bl'=4,'freq'=8] {'bl'}, use_global_device_ids=true, to_apply=%region_24.0 | all-reduce | flops 1 | bytes 8 | tf_op jit(solution)/shard_map/psum | solution.py:12
  244.1 10.8 %all-reduce = (f32[]{:T(128)}, f32[3,3]{0,1:T(4,128)S(1)}) all-reduce(f32[]{:T(128)} %psum.88, f32[3,3]{0,1:T(4,128)S(1)} %fusion.163), channel_id=1, replica_groups=mesh['bl'=4,'freq'=8] {'freq'}, use_global_device_ids=true, to_apply=%region_25.0 | all-reduce | flops 10 | bytes 80 | tf_op jit(solution)/shard_map/psum | solution.py:12
  256.6 10.9 %fusion.53 = (f32[8,16,2048]{2,1,0:T(8,128)S(1)}, f32[8,16,2048]{2,1,0:T(8,128)S(1)}, f32[8,16,2048]{2,1,0:T(8,128)S(1)}) fusion(f32[2,16,2048]{2,1,0:T(8,128)} %get-tuple-element.98, f32[2,16,2048]{2,1,0:T(8,128)} %get-tuple-element.97, f32[2,16,2048]{2,1,0:T(8,128)S(1)} %add_divide_fusion, f32[8,16,2048]{2,1,0:T(8,128)S(1)} %bitcast.268, ...), kind=kLoop, calls=%fused_computation.63 | loop fusion | flops 12845056 | bytes 6160960 | tf_op jit(solution)/shard_map/reduce_sum | solution.py:86
  269.4 3.0 fusion.1
  272.6 3.9 fusion.105
  280.4 22.4 %reduce-scatter.8.cloned.1.call-done = f32[3,8,16,128]{3,2,1,0:T(8,128)} async-done(((f32[3,8,16,512]{3,2,1,0:T(8,128)}), f32[3,8,16,128]{3,2,1,0:T(8,128)}) %reduce-scatter.8.cloned.1.call-update) | async-done | bytes 196624 | tf_op jit(solution)/shard_map/reduce_scatter | solution.py:204
  303.9 13.3 %all_gather.11 = f32[2,8,16,512]{3,2,1,0:T(8,128)S(1)} all-gather(f32[2,8,16,128]{3,2,1,0:T(8,128)S(1)} %pad_maximum_fusion.9), channel_id=1, replica_groups=mesh['bl'=4,'freq'=8] {'bl'}, dimensions={3}, use_global_device_ids=true | all-gather | bytes 655360 | tf_op jit(solution)/shard_map/all_gather | solution.py:214
  317.2 3.4 fusion
  320.5 3.4 fusion.7
  325.2 2.5 multiply_add_fusion
  327.7 8.9 %fusion.58 = (f32[2,16,2048]{2,1,0:T(8,128)S(1)}, f32[2,16,2048]{2,1,0:T(8,128)S(1)}) fusion(f32[8,16,2048]{2,1,0:T(8,128)S(1)} %bitcast.276, f32[8,16,2048]{2,1,0:T(8,128)S(1)} %bitcast.275, f32[16]{0:T(128)S(1)} %copy-done.30, f32[8,2,2048]{2,1,0:T(2,128)S(1)} %add_multiply_fusion, f32[8,16]{1,0:T(8,128)S(1)} %copy-done.28), kind=kLoop, calls=%fused_computation.68 | loop fusion | flops 5636096 | bytes 2753088 | tf_op jit(solution)/shard_map/reduce_sum | solution.py:58
  337.6 41.7 %all-reduce.5.cloned.1.call-done = f32[3,2,8,512]{3,2,1,0:T(8,128)} async-done(((f32[3,2,8,512]{3,2,1,0:T(8,128)}), f32[3,2,8,512]{3,2,1,0:T(8,128)}) %all-reduce.5.cloned.1.call-update) | async-done | bytes 98320 | tf_op jit(solution)/shard_map/psum | solution.py:225
  379.3 4.0 %subtract_divide_fusion = (f32[1,2,8,512]{3,2,1,0:T(8,128)S(1)}, f32[1,2,8,512]{3,2,1,0:T(8,128)S(1)}, f32[1,2,8,512]{3,2,1,0:T(8,128)S(1)}) fusion(f32[]{:T(128)} %bitcast.72, f32[]{:T(128)} %bitcast.69, f32[]{:T(128)} %bitcast.68, f32[3,2,8,512]{3,2,1,0:T(8,128)} %all-reduce.5.cloned.1.call-done, f32[]{:T(128)} %bitcast.71, f32[]{:T(128)} %bitcast.70, ...), kind=kLoop, calls=%fused_computation.253 | loop fusion | flops 139264 | bytes 196632 | tf_op jit(solution)/shard_map/div | solution.py:140
  (132 shorter events, 47.7 us)
Async XLA Ops:
  7.2 65.1 %copy-start = (f32[2,3,8,512]{3,2,1,0:T(8,128)S(1)}, f32[2,3,8,512]{3,2,1,0:T(8,128)}, u32[]{:S(2)}) copy-start(f32[2,3,8,512]{3,2,1,0:T(8,128)} %param.20) | copy-start | bytes 294916
  7.2 91.3 %reduce-scatter.4.cloned.1.call-start = ((), (), s32[]{:S(2)}) async-start(), calls=%async_computation.3 | async-start | bytes 983040 | tf_op jit(solution)/shard_map/reduce_scatter | solution.py:204
  8.0 3.2 copy-start.26
  11.3 2.1 copy-start.31
  13.4 2.6 copy-start.28
  13.5 2.5 copy-start.30
  15.8 9.2 %copy-start.2 = (f32[2,2,16,2048]{3,2,1,0:T(8,128)S(1)}, f32[2,2,16,2048]{3,2,1,0:T(8,128)}, u32[]{:S(2)}) copy-start(f32[2,2,16,2048]{3,2,1,0:T(8,128)} %param.11) | copy-start | bytes 1572868
  16.0 9.8 %copy-start.3 = (s32[2,16,2048]{2,1,0:T(8,128)S(1)}, s32[2,16,2048]{2,1,0:T(8,128)}, u32[]{:S(2)}) copy-start(s32[2,16,2048]{2,1,0:T(8,128)} %param.12) | copy-start | bytes 786436
  51.9 10.9 %copy-start.4 = (f32[128,2048]{1,0:T(8,128)S(1)}, f32[128,2048]{1,0:T(8,128)}, u32[]{:S(2)}) copy-start(f32[128,2048]{1,0:T(8,128)} %get-tuple-element.89) | copy-start | bytes 3145732
  51.9 10.9 %copy-start.5 = (f32[128,2048]{1,0:T(8,128)S(1)}, f32[128,2048]{1,0:T(8,128)}, u32[]{:S(2)}) copy-start(f32[128,2048]{1,0:T(8,128)} %get-tuple-element.90) | copy-start | bytes 3145732
  51.9 10.9 %copy-start.6 = (f32[128,2048]{1,0:T(8,128)S(1)}, f32[128,2048]{1,0:T(8,128)}, u32[]{:S(2)}) copy-start(f32[128,2048]{1,0:T(8,128)} %get-tuple-element.91) | copy-start | bytes 3145732
  51.9 10.9 %copy-start.7 = (f32[128,2048]{1,0:T(8,128)S(1)}, f32[128,2048]{1,0:T(8,128)}, u32[]{:S(2)}) copy-start(f32[128,2048]{1,0:T(8,128)} %get-tuple-element.92) | copy-start | bytes 3145732
  68.2 4.0 %copy-start.32 = (f32[8]{0:T(128)S(1)}, f32[8]{0:T(128)}, u32[]{:S(2)}) copy-start(f32[8]{0:T(128)} %param.21) | copy-start | bytes 100
  68.2 4.1 %copy-start.18 = (f32[2,8,16,512]{3,2,1,0:T(8,128)S(1)}, f32[2,8,16,512]{3,2,1,0:T(8,128)}, u32[]{:S(2)}) copy-start(f32[2,8,16,512]{3,2,1,0:T(8,128)} %param.19) | copy-start | bytes 1572868
  72.2 128.4 %reduce-scatter.6.cloned.1.call-start = ((), (), s32[]{:S(2)}) async-start(), calls=%async_computation.4 | async-start | bytes 983040 | tf_op jit(solution)/shard_map/reduce_scatter | solution.py:204
  73.3 41.6 %copy-start.24 = (f32[1,8,16,512]{3,2,1,0:T(8,128)}, f32[1,8,16,512]{3,2,1,0:T(8,128)S(1)}, u32[]{:S(2)}) copy-start(f32[1,8,16,512]{3,2,1,0:T(8,128)S(1)} %get-tuple-element.103) | copy-start | bytes 786436
  73.3 41.6 %copy-start.25 = (f32[1,8,16,512]{3,2,1,0:T(8,128)}, f32[1,8,16,512]{3,2,1,0:T(8,128)S(1)}, u32[]{:S(2)}) copy-start(f32[1,8,16,512]{3,2,1,0:T(8,128)S(1)} %get-tuple-element.104) | copy-start | bytes 786436
  112.7 2.1 copy-start.22
  154.4 11.0 %copy-start.12 = (f32[128,2048]{1,0:T(8,128)S(1)}, f32[128,2048]{1,0:T(8,128)}, u32[]{:S(2)}) copy-start(f32[128,2048]{1,0:T(8,128)} %get-tuple-element.81) | copy-start | bytes 3145732
  154.4 11.0 %copy-start.13 = (f32[128,2048]{1,0:T(8,128)S(1)}, f32[128,2048]{1,0:T(8,128)}, u32[]{:S(2)}) copy-start(f32[128,2048]{1,0:T(8,128)} %get-tuple-element.82) | copy-start | bytes 3145732
  154.4 11.0 %copy-start.14 = (f32[128,2048]{1,0:T(8,128)S(1)}, f32[128,2048]{1,0:T(8,128)}, u32[]{:S(2)}) copy-start(f32[128,2048]{1,0:T(8,128)} %get-tuple-element.83) | copy-start | bytes 3145732
  154.4 11.0 %copy-start.15 = (f32[128,2048]{1,0:T(8,128)S(1)}, f32[128,2048]{1,0:T(8,128)}, u32[]{:S(2)}) copy-start(f32[128,2048]{1,0:T(8,128)} %get-tuple-element.84) | copy-start | bytes 3145732
  170.4 4.2 %copy-start.23 = (f32[2,8,16,512]{3,2,1,0:T(8,128)S(1)}, f32[2,8,16,512]{3,2,1,0:T(8,128)}, u32[]{:S(2)}) copy-start(f32[2,8,16,512]{3,2,1,0:T(8,128)} %copy-done.22) | copy-start | bytes 1572868
  174.4 128.4 %reduce-scatter.8.cloned.1.call-start = ((), (), s32[]{:S(2)}) async-start(), calls=%async_computation.5 | async-start | bytes 983040 | tf_op jit(solution)/shard_map/reduce_scatter | solution.py:204
  256.6 11.0 %copy-start.8 = (f32[128,2048]{1,0:T(8,128)S(1)}, f32[128,2048]{1,0:T(8,128)}, u32[]{:S(2)}) copy-start(f32[128,2048]{1,0:T(8,128)} %get-tuple-element.73) | copy-start | bytes 3145732
  256.6 11.0 %copy-start.9 = (f32[128,2048]{1,0:T(8,128)S(1)}, f32[128,2048]{1,0:T(8,128)}, u32[]{:S(2)}) copy-start(f32[128,2048]{1,0:T(8,128)} %get-tuple-element.74) | copy-start | bytes 3145732
  256.6 11.0 %copy-start.10 = (f32[128,2048]{1,0:T(8,128)S(1)}, f32[128,2048]{1,0:T(8,128)}, u32[]{:S(2)}) copy-start(f32[128,2048]{1,0:T(8,128)} %get-tuple-element.75) | copy-start | bytes 3145732
  256.6 11.0 %copy-start.11 = (f32[128,2048]{1,0:T(8,128)S(1)}, f32[128,2048]{1,0:T(8,128)}, u32[]{:S(2)}) copy-start(f32[128,2048]{1,0:T(8,128)} %get-tuple-element.76) | copy-start | bytes 3145732
  272.6 7.7 %copy-start.21 = (f32[2,8,16,512]{3,2,1,0:T(8,128)S(1)}, f32[2,8,16,512]{3,2,1,0:T(8,128)}, u32[]{:S(2)}) copy-start(f32[2,8,16,512]{3,2,1,0:T(8,128)} %copy-done.20) | copy-start | bytes 1572868
  276.6 102.7 %all-reduce.5.cloned.1.call-start = ((), (), s32[]{:S(2)}) async-start(), calls=%async_computation.6 | async-start | bytes 196608 | tf_op jit(solution)/shard_map/psum | solution.py:225
  320.5 3.5 copy-start.19
  336.7 49.6 %copy-start.1 = (f32[2,3,8,512]{3,2,1,0:T(8,128)S(1)}, f32[2,3,8,512]{3,2,1,0:T(8,128)}, u32[]{:S(2)}) copy-start(f32[2,3,8,512]{3,2,1,0:T(8,128)} %param.20) | copy-start | bytes 294916
  (5 other events, 6.7 us)
Sparse Core Ops, SparseCore 0:
  72.3 26.1 reduce-scatter.3
  174.5 25.9 reduce-scatter.5
  276.7 26.0 reduce-scatter.7
  325.3 53.9 all-reduce.4
